TPU v7x, 32 devices: a whole 2x2x4 slice. The times are simulated.
32 devices in a mesh: seq: 16 (over z, x, core), head: 2 (over y).
Axes of the slice: x: 2, y: 2, z: 4, core: 2. Of those that a mesh axis runs over, the one named last changes fastest.
Arguments:
- query_rows: bfloat16 [8192, 1024], P(('seq', 'head')), may hold values from -16 to 16
- key_rows: bfloat16 [8192, 1024], P(('seq', 'head')), may hold values from -16 to 16
- value_rows: bfloat16 [8192, 1024], P(('seq', 'head')), may hold values from -6 to 6
- out_grad: bfloat16 [8192, 1024], P(('seq', 'head')), may hold values from -6 to 6
- random_blocks: int32 [128, 2], P('seq'), may hold values from 0 to 127, as said below
- global_blocks: int32 [2], replicated, may hold values from 0 to 127
Outputs:
- attn_out: bfloat16 [8192, 1024], P(('seq', 'head'))
- q_grad: bfloat16 [8192, 1024], P(('seq', 'head'))
- k_grad: bfloat16 [8192, 1024], P(('seq', 'head'))
- v_grad: bfloat16 [8192, 1024], P(('seq', 'head'))
Inputs may be any that keep to these rules, and one draw needn't show every extreme that they name: `random_blocks`: the 16 random blocks named by the query blocks of one device belong to 16 different devices along `seq`: at most one of them lies among any one device's 8 blocks.
All inputs are finite; a program needn't handle non-finite values.
Results may differ from a plain program's by a relative error of at most 0.011.
Values may be sent and summed in bfloat16 or wider, within the bound.
A program may use at most 128 MiB of HBM per device.

v0:
```python
from functools import partial

import jax
import jax.numpy as jnp
from jax import lax
from jax.experimental import pallas as pl
from jax.experimental.pallas import tpu as pltpu
from jax.sharding import PartitionSpec as P

HEAD_DIM = 64
BLOCK = 64
RANDOM = 2
GLOBALS = 2
PARTS = 3 + RANDOM + GLOBALS
MASKED = -1e30
MESH = pl.DeviceIdType.MESH
VMEM = pl.BlockSpec(memory_space=pltpu.VMEM)
HBM = pl.BlockSpec(memory_space=pltpu.HBM)
SMEM = pl.BlockSpec(memory_space=pltpu.SMEM)


def params(cid):
    return pltpu.CompilerParams(
        collective_id=cid, has_side_effects=True, vmem_limit_bytes=24 * 1024 * 1024
    )


def greet(n, heads):
    s, h = lax.axis_index("seq"), lax.axis_index("head")
    barrier = pltpu.get_barrier_semaphore()
    if n > 0:

        def hello(d, c):
            pl.semaphore_signal(
                barrier, inc=1, device_id={"seq": lax.rem(s + d, n)}, device_id_type=MESH
            )
            return c

        lax.fori_loop(1, n, hello, 0)
    for d in range(1, heads):
        pl.semaphore_signal(
            barrier, inc=1, device_id={"head": lax.rem(h + d, heads)}, device_id_type=MESH
        )
    pl.semaphore_wait(barrier, max(n - 1, 0) + heads - 1)


def cols(index, width, base=0):
    return pl.ds(pl.multiple_of(base + index * width, 128), width)


def rows(index, count):
    return pl.ds(pl.multiple_of(index * count, 16), count)


def each(n, f):
    def step(d, c):
        f(d)
        return c

    lax.fori_loop(1, n, step, 0)


def remote(src, dst, send, recv, **where):
    return pltpu.make_async_remote_copy(
        src_ref=src, dst_ref=dst, send_sem=send, recv_sem=recv, device_id=where,
        device_id_type=MESH,
    )


def exchange(view, heads, send, recv, local, base):
    h = lax.axis_index("head")
    copies = []
    for d in range(1, heads):
        peer = lax.rem(h + d, heads)
        source, target = view(h, peer)
        at = base * heads + d
        copies.append(remote(source, target, send.at[at], recv.at[at], head=peer))
    source, target = view(h, h)
    return copies + [pltpu.make_async_copy(source, target, local.at[base])]


def start(copies):
    for c in copies:
        c.start()


def wait(copies):
    for c in copies:
        c.wait()


def to_heads(src, dst, tokens, width):
    return lambda a, b: (src.at[:, cols(b, width)], dst.at[rows(a, tokens), :])


def piece_in(src, dst, width, offset, size):
    nt = src.shape[0]
    return lambda a, b: (
        src.at[:, :, pl.ds(pl.multiple_of(b * width + offset, 128), size)],
        dst.at[pl.ds(a * nt, nt)],
    )


def to_tokens(src, dst, tokens, width):
    return lambda a, b: (src.at[rows(b, tokens), :], dst.at[:, cols(a, width)])


def piece_out(src, dst, tokens, width, offset, size, base):
    return lambda a, b: (
        src.at[rows(b, tokens), pl.ds(base, size)],
        dst.at[:, pl.ds(pl.multiple_of(a * width + offset, 128), size)],
    )


def kernel_in(n, heads, size, key, ids, pair, ids_all, send, recv, local, isend, irecv):
    s = lax.axis_index("seq")
    greet(n, heads)
    copies = exchange(
        piece_in(key, pair, key.shape[2] // heads, 0, size), heads, send, recv, local, 0
    )

    def idc(d):
        return remote(ids, ids_all.at[s], isend.at[d], irecv.at[d], seq=lax.rem(s + d, n))

    mine = pltpu.make_async_copy(ids, ids_all.at[s], local.at[1])
    start(copies)
    each(n, lambda d: idc(d).start())
    mine.start()
    each(n, lambda d: idc(d).wait())
    mine.wait()
    wait(copies)


def halo(n, low, high, got, send, recv, at=0):
    s = lax.axis_index("seq")
    up, down = 2 * at, 2 * at + 1
    here = pl.ds(at * low.shape[1], low.shape[1])
    return [
        remote(high, got.at[0, :, here], send.at[up], recv.at[up], seq=lax.rem(s + 1, n)),
        remote(low, got.at[1, :, here], send.at[down], recv.at[down], seq=lax.rem(s + n - 1, n)),
    ]


def far_first(n, make):
    def go(i, c):
        make(n // 2 + ((i + 1) // 2) * (2 * lax.rem(i, 2) - 1)).start()
        return c

    lax.fori_loop(0, n - 1, go, 0)


def random_piece(n, c, src_of, dst, size, send, recv):
    s = lax.axis_index("seq")

    def make(d):
        peer = lax.rem(s + d, n)
        return remote(
            src_of(peer), dst.at[s, :, pl.ds(c * size, size)], send.at[c * n + d],
            recv.at[c * n + d], seq=peer,
        )

    return make


class Shared:
    def __init__(self, n, src, here, mine, layer, done, every, sems):
        s = lax.axis_index("seq")
        gs, gr, ls, lr, fs, fr, loc = sems
        self.group = group = src.shape[0]
        self.layers = n // group
        self.me, self.level = lax.rem(s, group), s // group
        self.mine, self.layer, self.done, self.every, self.here = mine, layer, done, every, here
        self.step1 = [pltpu.make_async_copy(src.at[self.me], here.at[self.me], loc.at[0])]
        self.step3 = []
        for j in range(1, group):
            to = lax.rem(self.me + j, group)
            peer = self.level * group + to
            self.step1.append(remote(src.at[to], here.at[self.me], gs.at[j], gr.at[j], seq=peer))
            self.step3.append(remote(done, every.at[self.me], fs.at[j], fr.at[j], seq=peer))
        self.across = lambda j: remote(
            mine, layer.at[self.level], ls.at[j], lr.at[j],
            seq=lax.rem(self.level + j, self.layers) * group + self.me,
        )

    def middle(self, combine):
        wait(self.step1)
        part = combine(self.here)
        self.mine[...] = part
        self.layer[self.level] = part
        each(self.layers, lambda j: self.across(j).start())

    def finish(self, combine):
        each(self.layers, lambda j: self.across(j).wait())
        total = combine(self.layer)
        self.done[...] = total
        self.every[self.me] = total
        start(self.step3)


def kernel_fetch(n, heads, pieces, served, owners, owned_at, query, grad, key, value, first, ready,
                 qh, gh, incoming, halos, gall, *rest):
    landed, rest = (first,) + rest[: pieces - 1], rest[pieces - 1 :]
    outgoing, gsrc, ghere, gmine, glayer, gdone = rest[:6]
    send, recv, local, bs, br, hs, hr, *gsems = rest[6:]
    s = lax.axis_index("seq")
    tokens, width = query.shape[0], query.shape[1] // heads
    size = 2 * width // pieces
    nb = first.shape[0]
    half = pieces // 2
    greet(n, heads)
    moves = [[]]
    for c in range(1, pieces):
        src = key if c < half else value
        moves.append(exchange(
            piece_in(src, landed[c], width, (c % half) * size, size),
            heads, send, recv, local, c,
        ))
    blocks = [
        random_piece(n, c, (lambda p, c=c: (ready.at[p] if c == 0 else outgoing.at[c - 1, p])),
                     incoming, size, bs, br)
        for c in range(pieces)
    ]
    qmove = exchange(to_heads(query, qh, tokens, width), heads, send, recv, local, pieces)
    qmove += exchange(to_heads(grad, gh, tokens, width), heads, send, recv, local, pieces + 1)
    edges = []
    for c in range(pieces):
        edges += halo(n, landed[c].at[0], landed[c].at[nb - 1], halos, hs, hr, c)
    shared = Shared(n, gsrc, ghere, gmine, glayer, gdone, gall, gsems)
    for m in moves:
        start(m)
    far_first(n, blocks[0])
    start(qmove)
    keep = pltpu.make_async_copy(ready.at[s], incoming.at[s, :, pl.ds(0, size)],
                                 local.at[pieces + 2])
    keep.start()
    for c in range(1, pieces):
        wait(moves[c])
        at = pl.ds(c * size, size)

        def gather(i, carry):
            outgoing[c - 1, i] = landed[c][served[i]]
            return carry

        lax.fori_loop(0, n, gather, 0)
        incoming[s, :, at] = landed[c][served[s]]
        if c == pieces - 1:
            group = gsrc.shape[0]
            per = group // GLOBALS
            count = BLOCK // per
            for m in range(group):
                low = (m % per) * count
                for k in range(pieces):
                    gsrc[m, :, pl.ds(k * size, size)] = landed[k][
                        owned_at[m // per], pl.ds(low, count), :
                    ]
            start(shared.step1 + edges)
            mine = owners[shared.me * GLOBALS // group]
            shared.middle(lambda ref: ref[lax.rem(mine, group)])
        far_first(n, blocks[c])
    shared.finish(lambda ref: ref[mine // group])
    keep.wait()
    wait(edges + qmove + shared.step3)
    for c in range(pieces):
        each(n, lambda d: blocks[c](d).wait())


def kernel_return(n, heads, pieces, served, owners, owned_at, att, qg, sending, edge, gsend, wsum,
                  out, qout, kout, vout, returned, halos, gall, summed, ghere, gmine, glayer,
                  gdone, send, recv, local, bs, br, hs, hr, *gsems):
    s = lax.axis_index("seq")
    width = att.shape[1]
    tokens = att.shape[0] // heads
    nb = att.shape[0] // BLOCK
    size = 2 * width // pieces
    half = pieces // 2
    greet(n, heads)
    moves = [
        exchange(
            piece_out(summed, kout if c < half else vout, tokens, width, (c % half) * size, size,
                      c * size),
            heads, send, recv, local, c,
        )
        for c in range(pieces)
    ]
    blocks = [
        random_piece(n, c, lambda p, c=c: sending.at[p, :, pl.ds(c * size, size)], returned, size,
                     bs, br)
        for c in range(pieces)
    ]
    qmove = exchange(to_tokens(att, out, tokens, width), heads, send, recv, local, pieces)
    qmove += exchange(to_tokens(qg, qout, tokens, width), heads, send, recv, local, pieces + 1)
    edges = halo(n, edge.at[0], edge.at[1], halos, hs, hr)
    shared = Shared(n, gsend, ghere, gmine, glayer, gdone, gall, gsems)
    keep = pltpu.make_async_copy(sending.at[s], returned.at[s], local.at[pieces + 2])

    def combine(ref):
        def add(i, acc):
            return acc + ref[i].astype(jnp.float32)

        zero = jnp.zeros(ref.shape[1:], jnp.float32)
        return lax.fori_loop(0, ref.shape[0], add, zero).astype(jnp.bfloat16)

    start(shared.step1 + edges)
    far_first(n, blocks[0])
    start(qmove + [keep])
    shared.middle(combine)
    for c in range(1, pieces):
        far_first(n, blocks[c])
    shared.finish(combine)
    keep.wait()
    wait(edges + shared.step3)
    strip = 16
    per = shared.group // GLOBALS
    count = BLOCK // per

    def weight(cond):
        return jnp.where(cond, 1.0, 0.0).astype(jnp.float32)

    for c in range(pieces):
        each(n, lambda d: blocks[c](d).wait())
        at = pl.ds(c * size, size)

        def one_strip(t, carry):
            low = pl.multiple_of(t * strip, strip)
            here = pl.ds(low, strip)
            acc = [wsum[pl.ds(pl.multiple_of((j + 1) * BLOCK + low, strip), strip), at]
                   for j in range(nb)]
            acc[0] = acc[0] + halos[0, here, at].astype(jnp.float32)
            acc[-1] = acc[-1] + halos[1, here, at].astype(jnp.float32)
            for g in range(GLOBALS):
                inside = pl.ds(pl.multiple_of(lax.rem(low, count), strip), strip)
                extra = gall[g * per + low // count, inside, at].astype(jnp.float32)
                for j in range(nb):
                    hit = (owners[g] == s) & (owned_at[g] == j)
                    acc[j] = acc[j] + weight(hit) * extra

            def add(i, accs):
                x = returned[i, here, at].astype(jnp.float32)
                which = served[i]
                return tuple(accs[j] + weight(which == j) * x for j in range(nb))

            acc = lax.fori_loop(0, n, add, tuple(acc))
            for j in range(nb):
                summed[pl.ds(pl.multiple_of(j * BLOCK + low, strip), strip), at] = acc[j].astype(
                    jnp.bfloat16
                )
            return carry

        lax.fori_loop(0, BLOCK // strip, one_strip, 0)
        start(moves[c])
    wait(qmove)
    for m in moves:
        wait(m)


def dot(a, b, ca, cb):
    return lax.dot_general(a, b, (((ca,), (cb,)), ((), ())), preferred_element_type=jnp.float32)


def kernel_attend(n, lanes, pieces, slots, qh, gh, halos, incoming, gall, *rest):
    landed, rest = rest[:pieces], rest[pieces:]
    att, qg, wsum, edge, sending, gsum, pairs, keys, gacc = rest
    nb = qh.shape[0] // BLOCK
    width = qh.shape[1]
    s = lax.axis_index("seq")
    per = lanes // HEAD_DIM
    scale = jnp.asarray(HEAD_DIM ** (-0.5), jnp.bfloat16)
    pairs[pl.ds(0, BLOCK)] = halos[0]
    size = landed[0].shape[1]
    for c in range(pieces):
        pairs[pl.ds(BLOCK, nb * BLOCK), pl.ds(c * size, size)] = landed[c][...]
    pairs[pl.ds((nb + 1) * BLOCK, BLOCK)] = halos[1]
    keys[pl.ds((3 + RANDOM) * BLOCK, GLOBALS * BLOCK)] = gall[...]
    gacc[...] = jnp.zeros_like(gacc)
    wsum[...] = jnp.zeros_like(wsum)
    if n > RANDOM * nb:
        sending[...] = jnp.zeros_like(sending)
    lane_head = lax.broadcasted_iota(jnp.int32, (BLOCK, lanes), 1) // HEAD_DIM
    part = lax.broadcasted_iota(jnp.int32, (PARTS * BLOCK, 1), 0) // BLOCK

    def stack(x):
        zero = jnp.zeros_like(x)
        return jnp.concatenate([jnp.where(lane_head == j, x, zero) for j in range(per)], axis=0)

    def unstack(x):
        got = x[0:BLOCK]
        for j in range(1, per):
            got = jnp.where(lane_head == j, x[j * BLOCK : (j + 1) * BLOCK], got)
        return got

    def block(b, carry):
        here = pl.ds(pl.multiple_of(b * BLOCK, BLOCK), BLOCK)
        window = pl.ds(pl.multiple_of(b * BLOCK, BLOCK), 3 * BLOCK)
        keys[pl.ds(0, 3 * BLOCK)] = pairs[window]
        for r in range(RANDOM):
            keys[pl.ds((3 + r) * BLOCK, BLOCK)] = incoming[slots[b * RANDOM + r]]
        number = s * nb + b
        bad = ((part == 0) & (number == 0)) | ((part == 2) & (number == n * nb - 1))
        for g in range(width // lanes):
            at = pl.ds(g * lanes, lanes)
            vat = pl.ds(width + g * lanes, lanes)
            q = stack(qh[here, at]) * scale
            do = stack(gh[here, at])
            k = keys[:, at]
            v = keys[:, vat]
            scores = jnp.where(bad, MASKED, dot(k, q, 1, 1))
            raw = jnp.exp(scores - jnp.max(scores, axis=0, keepdims=True))
            probs = raw * (1.0 / jnp.sum(raw, axis=0, keepdims=True))
            half = probs.astype(jnp.bfloat16)
            pgrad = dot(v, do, 1, 1)
            delta = jnp.sum(half.astype(jnp.float32) * pgrad, axis=0, keepdims=True)
            ds = (probs * (pgrad - delta)).astype(jnp.bfloat16)
            att[here, at] = unstack(dot(half, v, 0, 0)).astype(jnp.bfloat16)
            qg[here, at] = (unstack(dot(ds, k, 0, 0)) * HEAD_DIM ** (-0.5)).astype(jnp.bfloat16)
            for x, y, to in ((ds, q, at), (half, do, vat)):
                grad = dot(x, y, 1, 0)
                wsum[window, to] += grad[: 3 * BLOCK]
                for r in range(RANDOM):
                    low = (3 + r) * BLOCK
                    sending[slots[b * RANDOM + r], :, to] = grad[low : low + BLOCK].astype(
                        jnp.bfloat16
                    )
                gacc[:, to] += grad[(3 + RANDOM) * BLOCK :]
        return carry

    lax.fori_loop(0, nb, block, 0, unroll=2)
    edge[0] = wsum[pl.ds(0, BLOCK)].astype(jnp.bfloat16)
    edge[1] = wsum[pl.ds((nb + 1) * BLOCK, BLOCK)].astype(jnp.bfloat16)
    gsum[...] = gacc[...].astype(jnp.bfloat16)


def kernel_store(a, b, c, d, wa, wb, wc, wd, sem):
    copies = [
        pltpu.make_async_copy(x, y, sem.at[i])
        for i, (x, y) in enumerate(((a, wa), (b, wb), (c, wc), (d, wd)))
    ]
    start(copies)
    wait(copies)


def body(n, heads, query_rows, key_rows, value_rows, out_grad, random_blocks, global_blocks):
    bf = jnp.bfloat16
    tokens, full = query_rows.shape
    width = full // heads
    total = tokens * heads
    nb = total // BLOCK
    me = lax.axis_index("seq")
    dma = pltpu.SemaphoreType.DMA
    sds = jax.ShapeDtypeStruct
    requests = RANDOM * nb
    flat = random_blocks.reshape(requests)
    ids = jnp.broadcast_to(jnp.pad(flat, (0, 128 - requests))[None], (8, 128))
    pieces = min(4, 2 * width // 128)
    size = 2 * width // pieces
    blocked = (tokens // BLOCK, BLOCK, full)
    key_blocks, value_blocks = key_rows.reshape(blocked), value_rows.reshape(blocked)
    query_rows, key_blocks, value_blocks, out_grad = (
        pltpu.with_memory_space_constraint(x, pltpu.HBM)
        for x in (query_rows, key_blocks, value_blocks, out_grad)
    )
    first, ids_all = pl.pallas_call(
        partial(kernel_in, n, heads, size),
        out_shape=(sds((nb, BLOCK, size), bf), sds((n, 8, 128), jnp.int32)),
        in_specs=[HBM, VMEM],
        out_specs=(VMEM,) * 2,
        scratch_shapes=[dma((heads,)), dma((heads,)), dma((2,)), dma((n,)), dma((n,))],
        compiler_params=params(0),
        name="head_in",
    )(key_blocks, ids)
    asked = ids_all[:, 0, :requests]
    served = jnp.sum(jnp.where(asked // nb == me, asked % nb, 0), axis=1).astype(jnp.int32)
    owners = global_blocks // nb
    owned_at = global_blocks % nb
    ready = jnp.take(first, served, axis=0, mode="clip")
    group = 4
    layers = n // group
    chunk = GLOBALS * BLOCK // group
    slab = sds((n, BLOCK, 2 * width), bf)
    small = sds((group, chunk, 2 * width), bf)
    wide = (chunk, 2 * width)
    scratch = [
        pltpu.VMEM(small.shape, bf), pltpu.VMEM(wide, bf), pltpu.VMEM((layers,) + wide, bf),
        pltpu.VMEM(wide, bf),
        dma(((pieces + 2) * heads,)), dma(((pieces + 2) * heads,)), dma((pieces + 3,)),
        dma((pieces * n,)), dma((pieces * n,)), dma((2 * pieces,)), dma((2 * pieces,)),
        dma((group,)), dma((group,)), dma((layers,)), dma((layers,)), dma((group,)),
        dma((group,)), dma((1,)),
    ]
    edges = sds((2, BLOCK, 2 * width), bf)
    qh, gh, incoming, halos, gall, *landed = pl.pallas_call(
        partial(kernel_fetch, n, heads, pieces),
        out_shape=(sds((total, width), bf), sds((total, width), bf), slab, edges, small)
        + (sds((nb, BLOCK, size), bf),) * (pieces - 1),
        in_specs=[SMEM] * 3 + [HBM] * 4 + [VMEM] * 2,
        out_specs=(VMEM,) * (4 + pieces),
        scratch_shapes=[pltpu.VMEM((pieces - 1, n, BLOCK, size), bf), pltpu.VMEM(small.shape, bf)]
        + scratch,
        compiler_params=params(1),
        name="fetch",
    )(served, owners, owned_at, query_rows, out_grad, key_blocks, value_blocks, first, ready)
    gwide = (GLOBALS * BLOCK, 2 * width)
    att, qg, wsum, edge, sending, gsum = pl.pallas_call(
        partial(kernel_attend, n, min(256, width), pieces),
        out_shape=(
            sds((total, width), bf), sds((total, width), bf),
            sds(((nb + 2) * BLOCK, 2 * width), jnp.float32), edges, slab, sds(gwide, bf),
        ),
        in_specs=[SMEM] + [VMEM] * (5 + pieces),
        out_specs=(VMEM,) * 6,
        scratch_shapes=[
            pltpu.VMEM(((nb + 2) * BLOCK, 2 * width), bf),
            pltpu.VMEM((PARTS * BLOCK, 2 * width), bf),
            pltpu.VMEM(gwide, jnp.float32),
        ],
        compiler_params=pltpu.CompilerParams(vmem_limit_bytes=24 * 1024 * 1024),
        name="attend",
    )(flat // nb, qh, gh, halos, incoming, gall.reshape(gwide),
      *[x.reshape(total, size) for x in (first, *landed)])
    results = pl.pallas_call(
        partial(kernel_return, n, heads, pieces),
        out_shape=(sds((tokens, full), bf),) * 4,
        in_specs=[SMEM] * 3 + [VMEM] * 6,
        out_specs=(VMEM,) * 4,
        scratch_shapes=[
            pltpu.VMEM(slab.shape, bf), pltpu.VMEM(edges.shape, bf), pltpu.VMEM(small.shape, bf),
            pltpu.VMEM((total, 2 * width), bf),
        ] + scratch,
        compiler_params=params(2),
        name="give_back",
    )(served, owners, owned_at, att, qg, sending, edge, gsum.reshape(group, chunk, 2 * width),
      wsum)
    return pl.pallas_call(
        kernel_store,
        out_shape=(sds((tokens, full), bf),) * 4,
        in_specs=[VMEM] * 4,
        out_specs=(HBM,) * 4,
        scratch_shapes=[dma((4,))],
        compiler_params=pltpu.CompilerParams(vmem_limit_bytes=16 * 1024 * 1024),
        name="store",
    )(*results)


def solution(mesh):
    rows_spec = P(("seq", "head"), None)
    return jax.shard_map(
        partial(body, mesh.shape["seq"], mesh.shape["head"]),
        mesh=mesh,
        in_specs=(rows_spec,) * 4 + (P("seq", None), P()),
        out_specs=(rows_spec,) * 4,
        check_vma=False,
    )
```

profile of v0, /device:TPU:0, one launch (start us, length us, event | category | flops | bytes accessed | tf_op | source)
XLA Modules:
  0.0 150.7 jit_solution(7294747845570402407)
XLA Ops:
  0.6 0.7 and_select_fusion.1
  1.3 0.8 copy.11
  2.1 0.1 reshape.37
  2.2 11.9 %head_in.1 = (bf16[8,64,256]{2,1,0:T(8,128)(2,1)S(1)}, s32[16,8,128]{2,1,0:T(8,128)S(1)}) custom-call(bf16[4,64,1024]{2,1,0:T(8,128)(2,1)} %bitcast.15, s32[8,128]{1,0:T(8,128)S(1)} %broadcast_in_dim.12.ids), custom_call_target="tpu_custom_call" | custom-call | tf_op jit(solution)/shard_map/head_in/pallas_call | solution.py:461
  14.1 0.1 fusion.2.served
  14.2 0.6 gather_fusion
  14.8 58.1 %fetch.1 = (bf16[512,512]{1,0:T(8,128)(2,1)S(1)}, bf16[512,512]{1,0:T(8,128)(2,1)S(1)}, bf16[16,64,1024]{2,1,0:T(8,128)(2,1)S(1)}, bf16[2,64,1024]{2,1,0:T(8,128...) custom-call(s32[16]{0:T(128)S(1)} %fusion.2.served, ...), custom_call_target="tpu_custom_call" | custom-call | tf_op jit(solution)/shard_map/fetch/pallas_call | solution.py:490
  72.9 13.0 %attend.1 = (bf16[512,512]{1,0:T(8,128)(2,1)S(1)}, bf16[512,512]{1,0:T(8,128)(2,1)S(1)}, f32[640,1024]{1,0:T(8,128)S(1)}, bf16[2,64,1024]{2,1,0:T(8,128)(2,1)S(1...) custom-call(s32[16]{0:T(128)S(1)} %and_select_fusion.slots, ...), custom_call_target="tpu_custom_call" | custom-call | tf_op jit(solution)/shard_map/attend/pallas_call | solution.py:502
  85.9 63.4 %give_back.1 = (bf16[256,1024]{1,0:T(8,128)(2,1)S(1)}, bf16[256,1024]{1,0:T(8,128)(2,1)S(1)}, bf16[256,1024]{1,0:T(8,128)(2,1)S(1)}, bf16[256,1024]{1,0:T(8,128)(2,1)S(1)}) custom-call(s32[16]{0:T(128)S(1)} %fusion.2.served, s32[2]{0:T(128)S(1)} %get-tuple-element.45.owners, s32[2]{0:T(128)S(1)} %get-tuple-element.44.owned_at, ...), custom_call_target="tpu_custom_call" | custom-call | tf_op jit(solution)/shard_map/give_back/pallas_call | solution.py:519
  149.3 1.3 store.1
  (5 shorter events, 0.0 us)
where the time goes:
time: 151 us
  Pallas kernels  148 us (98%)
    pallas_call x1, Pallas kernels, body(): pl.pallas_call(partial(kernel_return, n, heads, pieces), out_shape=(sds((...  63.4 us
    pallas_call x1, Pallas kernels, body(): pl.pallas_call(partial(kernel_fetch, n, heads, pieces), out_shape=(sds((t...  58.1 us
    pallas_call x1, Pallas kernels, body(): pl.pallas_call(partial(kernel_attend, n, min(256, width), pieces), out_sh...  13 us
    pallas_call x1, Pallas kernels, body(): pl.pallas_call(partial(kernel_in, n, heads, size), out_shape=(sds((nb, BL...  11.9 us

commit v1 on v0

--- a/solution.py
+++ b/solution.py
@@ -540,10 +540,406 @@
     )(*results)
 
 
+LANES = 128
+WIDE = 2 * LANES
+
+
+class Team:
+    def __init__(self, n, heads, groups, tokens):
+        self.n, self.heads, self.groups, self.tokens = n, heads, groups, tokens
+        self.members = n // groups
+        s, self.h = lax.axis_index("seq"), lax.axis_index("head")
+        self.g, self.m = s // self.members, lax.rem(s, self.members)
+        self.bits = [1 << i for i in reversed(range(self.members.bit_length() - 1))]
+        self.places = [(i, d) for i in range(groups) for d in range(heads)]
+        self.me = self.slot(self.g, self.h)
+
+    def slot(self, g, h):
+        return g * self.heads + h
+
+    def near(self, i):
+        total = self.g * 0
+        for g in range(self.groups):
+            order = sorted(range(self.groups), key=lambda k: (abs(k - g), k))
+            total = total + jnp.where(self.g == g, order[i], 0)
+        return total
+
+    def place(self, j):
+        i, d = self.places[j]
+        return (self.near(i) if i else self.g), lax.rem(self.h + d, self.heads)
+
+    def device(self, g, h):
+        return {"seq": g * self.members + self.m, "head": h}
+
+    def mate(self, bit):
+        return self.m ^ bit
+
+    def mate_device(self, bit):
+        return {"seq": self.g * self.members + self.mate(bit)}
+
+    def chunk(self, g, h, m):
+        return rows((g * self.members + m) * self.heads + h, self.tokens)
+
+    def columns(self, g, h):
+        return pl.ds(pl.multiple_of((h * self.groups + g) * LANES, LANES), LANES)
+
+    def greet(self):
+        barrier = pltpu.get_barrier_semaphore()
+        for j in range(1, len(self.places)):
+            pl.semaphore_signal(
+                barrier, inc=1, device_id=self.device(*self.place(j)), device_id_type=MESH
+            )
+        for bit in self.bits:
+            pl.semaphore_signal(
+                barrier, inc=1, device_id=self.mate_device(bit), device_id_type=MESH
+            )
+        pl.semaphore_wait(barrier, len(self.places) - 1 + len(self.bits))
+
+
+def send_to(src, dst, send, recv, device):
+    return pltpu.make_async_remote_copy(
+        src_ref=src, dst_ref=dst, send_sem=send, recv_sem=recv, device_id=device,
+        device_id_type=MESH,
+    )
+
+
+def kernel_gather(n, heads, groups, key, value, query, grad, ids, kv, qd, ids_all, send, recv,
+                  local, fsend, frecv, isend, irecv):
+    tokens = query.shape[0]
+    t = Team(n, heads, groups, tokens)
+    count = len(t.places)
+    t.greet()
+    kvb = kv.at[pl.ds(BLOCK, kv.shape[0] - 2 * BLOCK)]
+
+    def move(a, j):
+        g, h = t.place(j)
+        src = (key, value, query, grad)[a].at[:, t.columns(g, h)]
+        lanes = pl.ds((a % 2) * LANES, LANES)
+        dst = (kvb.at[t.chunk(t.g, t.h, t.m), lanes] if a < 2
+               else qd.at[rows(t.me, tokens), lanes])
+        if j == 0:
+            return pltpu.make_async_copy(src, dst, local.at[a])
+        return send_to(src, dst, send.at[a * count + j], recv.at[a * count + t.me],
+                       t.device(g, h))
+
+    def arrived(a, j):
+        g, h = t.place(j)
+        src = (key, value, query, grad)[a].at[:, t.columns(g, h)]
+        lanes = pl.ds((a % 2) * LANES, LANES)
+        dst = (kvb.at[t.chunk(g, h, t.m), lanes] if a < 2
+               else qd.at[rows(t.slot(g, h), tokens), lanes])
+        return send_to(src, dst, send.at[a * count + j], recv.at[a * count + t.slot(g, h)],
+                       t.device(g, h))
+
+    idm = [send_to(ids, ids_all.at[t.g], isend.at[i], irecv.at[t.g], t.device(t.near(i), t.h))
+           for i in range(1, groups)]
+    idr = [send_to(ids, ids_all.at[t.near(i)], isend.at[i], irecv.at[t.near(i)],
+                   t.device(t.near(i), t.h)) for i in range(1, groups)]
+    start(idm)
+    for a in (0, 1):
+        for j in range(count):
+            move(a, j).start()
+    for a in (2, 3):
+        for j in range(count):
+            move(a, j).start()
+    mine = pltpu.make_async_copy(ids, ids_all.at[t.g], local.at[4])
+    mine.start()
+    edge = jnp.zeros((BLOCK, kv.shape[1]), kv.dtype)
+    kv[pl.ds(0, BLOCK)] = edge
+    kv[pl.ds(kv.shape[0] - BLOCK, BLOCK)] = edge
+
+    def forward(stage, mask, j, mine):
+        bit = t.bits[stage]
+        g, h = t.place(j)
+        owner = t.m ^ mask if mine else t.m ^ bit ^ mask
+        ref = kvb.at[t.chunk(g, h, owner)]
+        at = (stage * t.members + mask) * count + j
+        return send_to(ref, ref, fsend.at[at], frecv.at[at], t.mate_device(bit))
+
+    def masks(stage):
+        got = [0]
+        for bit in t.bits[:stage]:
+            got += [x ^ bit for x in got]
+        return got
+
+    lag = 1
+    stages = range(len(t.bits))
+    for step in range(count + lag * len(t.bits)):
+        for stage in reversed(stages):
+            j = step - lag * (stage + 1)
+            if 0 <= j < count:
+                for mask in masks(stage):
+                    forward(stage, mask, j, False).wait_recv()
+                    for later in range(stage + 1, len(t.bits)):
+                        forward(later, mask ^ t.bits[stage], j, True).start()
+        if step < count:
+            for a in (0, 1):
+                if step == 0:
+                    move(a, 0).wait()
+                else:
+                    arrived(a, step).wait_recv()
+            for stage in stages:
+                forward(stage, 0, step, True).start()
+    for stage in stages:
+        for mask in masks(stage):
+            for j in range(count):
+                forward(stage, mask, j, True).wait_send()
+    for a in (2, 3):
+        move(a, 0).wait()
+        for j in range(1, count):
+            arrived(a, j).wait_recv()
+    for a in range(4):
+        for j in range(1, count):
+            move(a, j).wait_send()
+    mine.wait()
+    for c in idr:
+        c.wait_recv()
+    for c in idm:
+        c.wait_send()
+
+
+def kernel_blocks(n, heads, groups, tokens, picks, owners, kv, qd, od, acc, part, keys, gacc):
+    t = Team(n, heads, groups, tokens)
+    run = tokens * heads // BLOCK
+    total = n * run
+    per = LANES // HEAD_DIM
+    scale = jnp.asarray(HEAD_DIM ** (-0.5), jnp.bfloat16)
+    acc[...] = jnp.zeros_like(acc)
+    gacc[...] = jnp.zeros_like(gacc)
+    for k in range(GLOBALS):
+        keys[pl.ds((3 + RANDOM + k) * BLOCK, BLOCK)] = kv[
+            pl.ds(pl.multiple_of((owners[k] + 1) * BLOCK, BLOCK), BLOCK)]
+    lane_head = lax.broadcasted_iota(jnp.int32, (BLOCK, LANES), 1) // HEAD_DIM
+    where = lax.broadcasted_iota(jnp.int32, (PARTS * BLOCK, 1), 0) // BLOCK
+    at, vat = pl.ds(0, LANES), pl.ds(LANES, LANES)
+
+    def stack(x):
+        zero = jnp.zeros_like(x)
+        return jnp.concatenate([jnp.where(lane_head == j, x, zero) for j in range(per)], axis=0)
+
+    def unstack(x):
+        got = x[0:BLOCK]
+        for j in range(1, per):
+            got = jnp.where(lane_head == j, x[j * BLOCK : (j + 1) * BLOCK], got)
+        return got
+
+    def block(b, carry):
+        here = pl.ds(pl.multiple_of(b * BLOCK, BLOCK), BLOCK)
+        number = ((b // run) * t.members + t.m) * run + lax.rem(b, run)
+        window = pl.ds(pl.multiple_of(number * BLOCK, BLOCK), 3 * BLOCK)
+        keys[pl.ds(0, 3 * BLOCK)] = kv[window]
+        picked = [pl.ds(pl.multiple_of((picks[b * RANDOM + r] + 1) * BLOCK, BLOCK), BLOCK)
+                  for r in range(RANDOM)]
+        for r in range(RANDOM):
+            keys[pl.ds((3 + r) * BLOCK, BLOCK)] = kv[picked[r]]
+        bad = ((where == 0) & (number == 0)) | ((where == 2) & (number == total - 1))
+        q = stack(qd[here, at]) * scale
+        do = stack(qd[here, vat])
+        k = keys[:, at]
+        v = keys[:, vat]
+        scores = jnp.where(bad, MASKED, dot(k, q, 1, 1))
+        raw = jnp.exp(scores - jnp.max(scores, axis=0, keepdims=True))
+        probs = raw * (1.0 / jnp.sum(raw, axis=0, keepdims=True))
+        half = probs.astype(jnp.bfloat16)
+        pgrad = dot(v, do, 1, 1)
+        delta = jnp.sum(half.astype(jnp.float32) * pgrad, axis=0, keepdims=True)
+        ds = (probs * (pgrad - delta)).astype(jnp.bfloat16)
+        od[here, at] = unstack(dot(half, v, 0, 0)).astype(jnp.bfloat16)
+        od[here, vat] = (unstack(dot(ds, k, 0, 0)) * HEAD_DIM ** (-0.5)).astype(jnp.bfloat16)
+        for x, y, to in ((ds, q, at), (half, do, vat)):
+            out = dot(x, y, 1, 0)
+            acc[window, to] += out[: 3 * BLOCK]
+            for r in range(RANDOM):
+                low = (3 + r) * BLOCK
+                acc[picked[r], to] += out[low : low + BLOCK]
+            gacc[:, to] += out[(3 + RANDOM) * BLOCK :]
+        return carry
+
+    lax.fori_loop(0, qd.shape[0] // BLOCK, block, 0, unroll=2)
+    for k in range(GLOBALS):
+        acc[pl.ds(pl.multiple_of((owners[k] + 1) * BLOCK, BLOCK), BLOCK)] += gacc[
+            pl.ds(k * BLOCK, BLOCK)]
+
+    def convert(i, carry):
+        part[rows(i, BLOCK)] = acc[rows(i + 1, BLOCK)].astype(jnp.bfloat16)
+        return carry
+
+    lax.fori_loop(0, total, convert, 0)
+
+
+def kernel_scatter(n, heads, groups, od, acc, part, out, qout, kout, vout, inbox, sums, final,
+                   send, recv, local, fsend, frecv):
+    tokens = out.shape[0]
+    t = Team(n, heads, groups, tokens)
+    count = len(t.places)
+    t.greet()
+    mine = t.columns(t.g, t.h)
+    dests = (out, qout, kout, vout)
+
+    def lanes(a):
+        return pl.ds((a % 2) * LANES, LANES)
+
+    def move(a, j):
+        g, h = t.place(j)
+        base = od if a < 2 else final
+        src = base.at[rows(t.slot(g, h) if a < 2 else j, tokens), lanes(a)]
+        dst = dests[a].at[:, mine]
+        if j == 0:
+            return pltpu.make_async_copy(src, dst, local.at[a])
+        return send_to(src, dst, send.at[a * count + j], recv.at[a * count + t.me],
+                       t.device(g, h))
+
+    def arrived(a, j):
+        g, h = t.place(j)
+        base = od if a < 2 else final
+        src = base.at[rows(t.slot(g, h) if a < 2 else j, tokens), lanes(a)]
+        return send_to(src, dests[a].at[:, t.columns(g, h)], send.at[a * count + j],
+                       recv.at[a * count + t.slot(g, h)], t.device(g, h))
+
+    order = list(reversed(t.bits))
+    owners = []
+    held = list(range(t.members))
+    for bit in order:
+        owners.append([x for x in held if x & bit])
+        held = [x for x in held if not x & bit]
+
+    def trade(stage, mask, j, src):
+        at = (stage * t.members + mask) * count + j
+        return send_to(src, inbox.at[rows(at_box(stage, mask, j), tokens)], fsend.at[at],
+                       frecv.at[at], t.mate_device(order[stage]))
+
+    boxes = [(stage, mask) for stage in range(len(order)) for mask in owners[stage]]
+
+    def at_box(stage, mask, j):
+        return boxes.index((stage, mask)) * count + j
+
+    def chunk_of(mask, j):
+        g, h = t.place(j)
+        return t.chunk(g, h, t.m ^ mask)
+
+    def below(ref):
+        return pl.ds(BLOCK + ref.start, ref.size)
+
+    js = list(range(1, count)) + [0]
+    for j in js:
+        for mask in reversed(owners[0]):
+            trade(0, mask, j, part.at[chunk_of(mask, j)]).start()
+    for a in (0, 1):
+        for j in range(count):
+            move(a, j).start()
+
+    def total(mask, j, upto):
+        x = acc[below(chunk_of(mask, j))]
+        for stage in range(upto):
+            full = mask ^ order[stage]
+            x = x + inbox[rows(at_box(stage, full, j), tokens)].astype(jnp.float32)
+        return x.astype(jnp.bfloat16)
+
+    sent = [(0, mask, j, None) for mask in owners[0] for j in js]
+    for stage in range(1, len(order)):
+        for j in js:
+            for mask in owners[stage]:
+                for before in range(stage):
+                    trade(before, mask ^ order[before], j, inbox.at[rows(0, tokens)]).wait_recv()
+                spot = rows((stage - 1) * count + j, tokens)
+                sums[spot] = total(mask, j, stage)
+                trade(stage, mask, j, sums.at[spot]).start()
+    for j in js:
+        for stage in range(len(order)):
+            trade(stage, order[stage], j, inbox.at[rows(0, tokens)]).wait_recv()
+        final[rows(j, tokens)] = total(0, j, len(order))
+        for a in (2, 3):
+            move(a, j).start()
+    for stage in range(len(order)):
+        for mask in owners[stage]:
+            for j in js:
+                trade(stage, mask, j, inbox.at[rows(0, tokens)]).wait_send()
+    for a in range(4):
+        move(a, 0).wait()
+        for j in range(1, count):
+            move(a, j).wait_send()
+            arrived(a, j).wait_recv()
+
+
+def grouped(n, heads, groups, query_rows, key_rows, value_rows, out_grad, random_blocks,
+            global_blocks):
+    bf = jnp.bfloat16
+    tokens, full = query_rows.shape
+    members = n // groups
+    count = groups * heads
+    everything = n * heads * tokens
+    held = count * tokens
+    bits = members.bit_length() - 1
+    requests = random_blocks.size
+    dma = pltpu.SemaphoreType.DMA
+    sds = jax.ShapeDtypeStruct
+    ids = jnp.pad(random_blocks.reshape(1, requests), ((0, 7), (0, 128 - requests)))
+    query_rows, key_rows, value_rows, out_grad = (
+        pltpu.with_memory_space_constraint(x, pltpu.HBM)
+        for x in (query_rows, key_rows, value_rows, out_grad)
+    )
+    kv, qd, ids_all = pl.pallas_call(
+        partial(kernel_gather, n, heads, groups),
+        out_shape=(sds((everything + 2 * BLOCK, WIDE), bf), sds((held, WIDE), bf),
+                   sds((groups, 8, 128), jnp.int32)),
+        in_specs=[HBM] * 4 + [VMEM],
+        out_specs=(VMEM,) * 3,
+        scratch_shapes=[dma((4 * count,)), dma((4 * count,)), dma((5,)),
+                        dma((bits * members * count,)), dma((bits * members * count,)),
+                        dma((groups,)), dma((groups,))],
+        compiler_params=params(0),
+        name="gather",
+    )(key_rows, value_rows, query_rows, out_grad, ids)
+    picks = ids_all[:, 0, :requests].reshape(groups * requests)
+    od, acc, part = pl.pallas_call(
+        partial(kernel_blocks, n, heads, groups, tokens),
+        out_shape=(sds((held, WIDE), bf), sds((everything + 2 * BLOCK, WIDE), jnp.float32),
+                   sds((everything, WIDE), bf)),
+        in_specs=[SMEM] * 2 + [VMEM] * 2,
+        out_specs=(VMEM,) * 3,
+        scratch_shapes=[pltpu.VMEM((PARTS * BLOCK, WIDE), bf),
+                        pltpu.VMEM((GLOBALS * BLOCK, WIDE), jnp.float32)],
+        compiler_params=pltpu.CompilerParams(vmem_limit_bytes=24 * 1024 * 1024),
+        name="blocks",
+    )(picks, global_blocks, kv, qd)
+    results = pl.pallas_call(
+        partial(kernel_scatter, n, heads, groups),
+        out_shape=(sds((tokens, full), bf),) * 4,
+        in_specs=[VMEM] * 3,
+        out_specs=(VMEM,) * 4,
+        scratch_shapes=[
+            pltpu.VMEM(((members - 1) * held, WIDE), bf),
+            pltpu.VMEM((max(bits - 1, 1) * held, WIDE), bf), pltpu.VMEM((held, WIDE), bf),
+            dma((4 * count,)), dma((4 * count,)), dma((4,)),
+            dma((bits * members * count,)), dma((bits * members * count,)),
+        ],
+        compiler_params=params(1),
+        name="scatter",
+    )(od, acc, part)
+    return pl.pallas_call(
+        kernel_store,
+        out_shape=(sds((tokens, full), bf),) * 4,
+        in_specs=[VMEM] * 4,
+        out_specs=(HBM,) * 4,
+        scratch_shapes=[dma((4,))],
+        compiler_params=pltpu.CompilerParams(vmem_limit_bytes=16 * 1024 * 1024),
+        name="store",
+    )(*results)
+
+
+def chosen(n, heads, query_rows, *others):
+    tokens, full = query_rows.shape
+    groups = full // LANES // heads
+    fits = n * heads * tokens * WIDE * 6 <= 24 * 1024 * 1024
+    if full % (LANES * heads) == 0 and n % groups == 0 and fits and n // groups in (2, 4):
+        return grouped(n, heads, groups, query_rows, *others)
+    return body(n, heads, query_rows, *others)
+
+
 def solution(mesh):
     rows_spec = P(("seq", "head"), None)
     return jax.shard_map(
-        partial(body, mesh.shape["seq"], mesh.shape["head"]),
+        partial(chosen, mesh.shape["seq"], mesh.shape["head"]),
         mesh=mesh,
         in_specs=(rows_spec,) * 4 + (P("seq", None), P()),
         out_specs=(rows_spec,) * 4,

time: 151 us -> 140 us (0.927)
  Pallas kernels: 148 us -> 133 us
  local copies, waits for them, and re-layouts: 1.43 us -> 5.76 us
    pallas_call x5 -> x4, Pallas kernels: 148 us -> 133 us  [the longest x1 58.6 us: grouped(): pl.pallas_call(partial(kernel_gather, n, heads, groups), out_shape=(sds((...]
    unnamed x1 -> x7, local copies, waits for them, and re-layouts: 0.75 us -> 5.57 us
where the time goes in v1:
time: 140 us
  Pallas kernels  133 us (95%)
  local copies, waits for them, and re-layouts  5.76 us (4%)
    pallas_call x1, Pallas kernels, grouped(): pl.pallas_call(partial(kernel_gather, n, heads, groups), out_shape=(sds((...  58.6 us
    pallas_call x1, Pallas kernels, grouped(): pl.pallas_call(partial(kernel_scatter, n, heads, groups), out_shape=(sds(...  51.7 us
    pallas_call x1, Pallas kernels, grouped(): pl.pallas_call(partial(kernel_blocks, n, heads, groups, tokens), out_shap...  21.7 us
    unnamed x7, local copies, waits for them, and re-layouts  5.57 us

profile of v1, /device:TPU:0, one launch (start us, length us, event | category | flops | bytes accessed | tf_op | source)
XLA Modules:
  0.0 139.8 jit_solution(13660896992701622540)
XLA Ops:
  0.6 0.8 copy.11
  1.4 0.1 reshape.11
  1.5 58.6 %gather.1 = (bf16[8320,256]{1,0:T(8,128)(2,1)S(1)}, bf16[2048,256]{1,0:T(8,128)(2,1)S(1)}, s32[4,8,128]{2,1,0:T(8,128)S(1)}) custom-call(bf16[256,1024]{1,0:T(8,128)(2,1)} %key.1, bf16[256,1024]{1,0:T(8,128)(2,1)} %value.1, bf16[256,1024]{1,0:T(8,128)(2,1)} %query.1, bf16[256,1024]{1,0:T(8,128)(2,1)} %grad.1, s32[8,128]{1,0:T(8,128)S(1)} %pad.4.ids), custom_call_target="tpu_custom_call" | custom-call | tf_op jit(solution)/shard_map/gather/pallas_call | solution.py:881
  60.1 0.0 copy-start
  60.1 2.0 %copy-done = bf16[8320,256]{1,0:T(8,128)(2,1)} copy-done((bf16[8320,256]{1,0:T(8,128)(2,1)}, bf16[8320,256]{1,0:T(8,128)(2,1)S(1)}, u32[]{:S(2)}) %copy-start) | copy-done | bytes 4259864
  62.1 0.1 reshape_squeeze.3.picks
  62.2 0.0 copy-start.1
  62.2 2.2 %copy-done.1 = bf16[8320,256]{1,0:T(8,128)(2,1)S(1)} copy-done((bf16[8320,256]{1,0:T(8,128)(2,1)S(1)}, bf16[8320,256]{1,0:T(8,128)(2,1)}, u32[]{:S(2)}) %copy-start.1) | copy-done | bytes 4259864
  64.4 0.0 copy-start.2
  64.4 0.7 copy-done.2
  65.0 21.7 %blocks.1 = (bf16[2048,256]{1,0:T(8,128)(2,1)S(1)}, f32[8320,256]{1,0:T(8,128)S(1)}, bf16[8192,256]{1,0:T(8,128)(2,1)S(1)}) custom-call(s32[64]{0:T(128)S(1)} %reshape_squeeze.3.picks, s32[2]{0:T(128)S(1)} %copy-done.2, bf16[8320,256]{1,0:T(8,128)(2,1)S(1)} %copy-done.1, bf16[2048,256]{1,0:T(8,128)(2,1)S(1)} %get-tuple-element.16.qd), custom_call_target="tpu_custom_call" | custom-call | tf_op jit(solution)/shard_map/blocks/pallas_call | solution.py:894
  86.7 51.7 %scatter.1 = (bf16[256,1024]{1,0:T(8,128)(2,1)S(1)}, bf16[256,1024]{1,0:T(8,128)(2,1)S(1)}, bf16[256,1024]{1,0:T(8,128)(2,1)S(1)}, bf16[256,1024]{1,0:T(8,128)(2,1)S(1)}) custom-call(bf16[2048,256]{1,0:T(8,128)(2,1)S(1)} %get-tuple-element.17.od, f32[8320,256]{1,0:T(8,128)S(1)} %get-tuple-element.18.acc, bf16[8192,256]{1,0:T(8,128)(2,1)S(1)} %get-tuple-element.19.part), custom_call_target="tpu_custom_call" | custom-call | tf_op jit(solution)/shard_map/scatter/pallas_call | solution.py:905
  138.4 1.3 store.1
  (2 shorter events, 0.0 us)
Async XLA Ops:
  60.1 2.0 %copy-start = (bf16[8320,256]{1,0:T(8,128)(2,1)}, bf16[8320,256]{1,0:T(8,128)(2,1)S(1)}, u32[]{:S(2)}) copy-start(bf16[8320,256]{1,0:T(8,128)(2,1)S(1)} %get-tuple-element.15.kv) | copy-start | bytes 12779524
  62.2 2.2 %copy-start.1 = (bf16[8320,256]{1,0:T(8,128)(2,1)S(1)}, bf16[8320,256]{1,0:T(8,128)(2,1)}, u32[]{:S(2)}) copy-start(bf16[8320,256]{1,0:T(8,128)(2,1)} %copy-done) | copy-start | bytes 12779524
  64.4 0.7 copy-start.2

commit v2 on v0

--- a/solution.py
+++ b/solution.py
@@ -540,10 +540,431 @@
     )(*results)
 
 
+LANES = 128
+WIDE = 2 * LANES
+
+
+class Team:
+    def __init__(self, n, heads, groups, tokens):
+        self.n, self.heads, self.groups, self.tokens = n, heads, groups, tokens
+        self.members = n // groups
+        s, self.h = lax.axis_index("seq"), lax.axis_index("head")
+        self.g, self.m = s // self.members, lax.rem(s, self.members)
+        self.bits = [1 << i for i in reversed(range(self.members.bit_length() - 1))]
+        self.places = [(i, d) for i in range(groups) for d in range(heads)]
+        self.me = self.slot(self.g, self.h)
+
+    def slot(self, g, h):
+        return g * self.heads + h
+
+    def near(self, i):
+        total = self.g * 0
+        for g in range(self.groups):
+            order = sorted(range(self.groups), key=lambda k: (abs(k - g), k))
+            total = total + jnp.where(self.g == g, order[i], 0)
+        return total
+
+    def place(self, j):
+        if isinstance(j, int):
+            i, d = self.places[j]
+            return (self.near(i) if i else self.g), lax.rem(self.h + d, self.heads)
+        g = self.g * 0
+        for i in range(self.groups):
+            g = g + jnp.where(j // self.heads == i, self.near(i), 0)
+        return g, lax.rem(self.h + lax.rem(j, self.heads), self.heads)
+
+    def device(self, g, h):
+        return {"seq": g * self.members + self.m, "head": h}
+
+    def mate(self, bit):
+        return self.m ^ bit
+
+    def mate_device(self, bit):
+        return {"seq": self.g * self.members + self.mate(bit)}
+
+    def chunk(self, g, h, m):
+        return rows((g * self.members + m) * self.heads + h, self.tokens)
+
+    def columns(self, g, h):
+        return pl.ds(pl.multiple_of((h * self.groups + g) * LANES, LANES), LANES)
+
+    def greet(self):
+        barrier = pltpu.get_barrier_semaphore()
+        for j in range(1, len(self.places)):
+            pl.semaphore_signal(
+                barrier, inc=1, device_id=self.device(*self.place(j)), device_id_type=MESH
+            )
+        for bit in self.bits:
+            pl.semaphore_signal(
+                barrier, inc=1, device_id=self.mate_device(bit), device_id_type=MESH
+            )
+        pl.semaphore_wait(barrier, len(self.places) - 1 + len(self.bits))
+
+
+def send_to(src, dst, send, recv, device):
+    return pltpu.make_async_remote_copy(
+        src_ref=src, dst_ref=dst, send_sem=send, recv_sem=recv, device_id=device,
+        device_id_type=MESH,
+    )
+
+
+def kernel_all(n, heads, groups, owners, key, value, query, grad, ids, out, qout, kout, vout,
+               kv, qd, od, acc, extra, keys, ids_all, table, part, inbox, sums, final, send, recv,
+               local, fsend, frecv, isend, irecv, bsend, brecv, blocal, tsend, trecv):
+    tokens = query.shape[0]
+    t = Team(n, heads, groups, tokens)
+    count = len(t.places)
+    per_chunk = tokens // BLOCK
+    run = heads * per_chunk
+    requests = RANDOM * run
+    t.greet()
+    arrays = (key, value, query, grad)
+    dests = (out, qout, kout, vout)
+
+    def lanes(a):
+        return pl.ds((a % 2) * LANES, LANES)
+
+    def blocks_of(g, h, m):
+        return pl.ds(((g * t.members + m) * heads + h) * per_chunk + 1, per_chunk)
+
+    def leaving(a, g, h):
+        ref = arrays[a]
+        return ref.at[:, :, t.columns(g, h)] if a < 2 else ref.at[:, t.columns(g, h)]
+
+    def landing(a, g, h):
+        return (kv.at[blocks_of(g, h, t.m), :, lanes(a)] if a < 2
+                else qd.at[rows(t.slot(g, h), tokens), lanes(a)])
+
+    def move(a, j):
+        g, h = t.place(j)
+        return send_to(leaving(a, g, h), landing(a, t.g, t.h),
+                       send.at[a * count + j], recv.at[a * count + t.me], t.device(g, h))
+
+    def keep(a):
+        return pltpu.make_async_copy(leaving(a, t.g, t.h), landing(a, t.g, t.h),
+                                     local.at[a])
+
+    def arrived(a, j):
+        g, h = t.place(j)
+        return send_to(leaving(a, g, h), landing(a, g, h),
+                       send.at[a * count + j], recv.at[a * count + t.slot(g, h)],
+                       t.device(g, h))
+
+    idm = [send_to(ids, ids_all.at[t.g], isend.at[i], irecv.at[t.g], t.device(t.near(i), t.h))
+           for i in range(1, groups)]
+    idr = [send_to(ids, ids_all.at[t.near(i)], isend.at[i], irecv.at[t.near(i)],
+                   t.device(t.near(i), t.h)) for i in range(1, groups)]
+    for a in (0, 1):
+        keep(a).start()
+        for j in range(1, count):
+            move(a, j).start()
+    start(idm)
+    for a in (2, 3):
+        keep(a).start()
+        for j in range(1, count):
+            move(a, j).start()
+    own = pltpu.make_async_copy(ids, ids_all.at[t.g], local.at[4])
+    own.start()
+    edge = jnp.zeros(kv.shape[1:], kv.dtype)
+    kv[0] = edge
+    kv[kv.shape[0] - 1] = edge
+    empty = jnp.zeros((BLOCK, WIDE), jnp.float32)
+    for k in range(GLOBALS + 1):
+        extra[groups * requests + k] = empty
+
+    def clear(i, carry):
+        acc[rows(i, BLOCK)] = empty
+        return carry
+
+    lax.fori_loop(0, acc.shape[0] // BLOCK, clear, 0)
+
+    def forward(stage, mask, j, mine):
+        bit = t.bits[stage]
+        g, h = t.place(j)
+        owner = t.m ^ mask if mine else t.m ^ bit ^ mask
+        ref = kv.at[blocks_of(g, h, owner)]
+        at = (stage * t.members + mask) * count + j
+        return send_to(ref, ref, fsend.at[at], frecv.at[at], t.mate_device(bit))
+
+    def masks(stage):
+        got = [0]
+        for bit in t.bits[:stage]:
+            got += [x ^ bit for x in got]
+        return got
+
+    stages = range(len(t.bits))
+    for step in range(count + len(t.bits)):
+        for stage in reversed(stages):
+            j = step - stage - 1
+            if 0 <= j < count:
+                for mask in masks(stage):
+                    forward(stage, mask, j, False).wait_recv()
+                    for later in range(stage + 1, len(t.bits)):
+                        forward(later, mask ^ t.bits[stage], j, True).start()
+        if step < count:
+            for a in (0, 1):
+                if step == 0:
+                    keep(a).wait()
+                else:
+                    arrived(a, step).wait_recv()
+            for stage in stages:
+                forward(stage, 0, step, True).start()
+    own.wait()
+    for c in idr:
+        c.wait_recv()
+    fill = pltpu.make_async_copy(ids_all, table, local.at[5])
+    fill.start()
+    fill.wait()
+
+    per = LANES // HEAD_DIM
+    scale = jnp.asarray(HEAD_DIM ** (-0.5), jnp.bfloat16)
+    for k in range(GLOBALS):
+        keys[3 + RANDOM + k] = kv[owners[k] + 1]
+    lane_head = lax.broadcasted_iota(jnp.int32, (BLOCK, LANES), 1) // HEAD_DIM
+    where = lax.broadcasted_iota(jnp.int32, (PARTS * BLOCK, 1), 0) // BLOCK
+    at, vat = lanes(0), lanes(1)
+
+    def stack(x):
+        zero = jnp.zeros_like(x)
+        return jnp.concatenate([jnp.where(lane_head == j, x, zero) for j in range(per)], axis=0)
+
+    def unstack(x):
+        got = x[0:BLOCK]
+        for j in range(1, per):
+            got = jnp.where(lane_head == j, x[j * BLOCK : (j + 1) * BLOCK], got)
+        return got
+
+    def chunk(j):
+        g, h = t.place(j)
+        slot = t.slot(g, h)
+        first = ((g * t.members + t.m) * heads + h) * per_chunk
+
+        def block(b, carry):
+            here = rows(slot * per_chunk + b, BLOCK)
+            number = first + b
+            window = pl.ds(pl.multiple_of(number * BLOCK, BLOCK), 3 * BLOCK)
+            keys[pl.ds(0, 3)] = kv[pl.ds(number, 3)]
+            spot = (h * per_chunk + b) * RANDOM
+            for r in range(RANDOM):
+                keys[3 + r] = kv[table[g, 0, spot + r] + 1]
+            bad = ((where == 0) & (number == 0)) | ((where == 2) & (number == n * run - 1))
+            q = stack(qd[here, at]) * scale
+            do = stack(qd[here, vat])
+            k = keys[:, :, at].reshape(PARTS * BLOCK, LANES)
+            v = keys[:, :, vat].reshape(PARTS * BLOCK, LANES)
+            scores = jnp.where(bad, MASKED, dot(k, q, 1, 1))
+            raw = jnp.exp(scores - jnp.max(scores, axis=0, keepdims=True))
+            probs = raw * (1.0 / jnp.sum(raw, axis=0, keepdims=True))
+            half = probs.astype(jnp.bfloat16)
+            pgrad = dot(v, do, 1, 1)
+            delta = jnp.sum(half.astype(jnp.float32) * pgrad, axis=0, keepdims=True)
+            ds = (probs * (pgrad - delta)).astype(jnp.bfloat16)
+            od[here, at] = unstack(dot(half, v, 0, 0)).astype(jnp.bfloat16)
+            od[here, vat] = (unstack(dot(ds, k, 0, 0)) * HEAD_DIM ** (-0.5)).astype(jnp.bfloat16)
+            for x, y, to in ((ds, q, at), (half, do, vat)):
+                got = dot(x, y, 1, 0)
+                acc[window, to] += got[: 3 * BLOCK]
+                for r in range(RANDOM):
+                    low = (3 + r) * BLOCK
+                    extra[g * requests + spot + r, :, to] = got[low : low + BLOCK]
+                for k2 in range(GLOBALS):
+                    low = (3 + RANDOM + k2) * BLOCK
+                    extra[groups * requests + k2, :, to] += got[low : low + BLOCK]
+            return carry
+
+        lax.fori_loop(0, per_chunk, block, 0, unroll=2)
+
+    mine = t.columns(t.g, t.h)
+
+    def source(a, j):
+        g, h = t.place(j)
+        return (od.at[rows(t.slot(g, h), tokens), lanes(a)] if a < 2
+                else final.at[rows(j, tokens), lanes(a)])
+
+    def back(a, j):
+        g, h = t.place(j)
+        return send_to(source(a, j), dests[a].at[:, mine], bsend.at[a * count + j],
+                       brecv.at[a * count + t.me], t.device(g, h))
+
+    def back_keep(a):
+        return pltpu.make_async_copy(source(a, 0), dests[a].at[:, mine], blocal.at[a])
+
+    def returned(a, j):
+        g, h = t.place(j)
+        return send_to(source(a, j), dests[a].at[:, t.columns(g, h)], bsend.at[a * count + j],
+                       brecv.at[a * count + t.slot(g, h)], t.device(g, h))
+
+    for a in (2, 3):
+        keep(a).wait()
+    chunk(0)
+    for a in (0, 1):
+        back_keep(a).start()
+
+    def one(j, carry):
+        for a in (2, 3):
+            arrived(a, j).wait_recv()
+        chunk(j)
+        for a in (0, 1):
+            back(a, j).start()
+        return carry
+
+    lax.fori_loop(1, count, one, 0)
+
+    order = list(reversed(t.bits))
+    handed = []
+    held = list(range(t.members))
+    for bit in order:
+        handed.append([x for x in held if x & bit])
+        held = [x for x in held if not x & bit]
+    boxes = [(stage, mask) for stage in range(len(order)) for mask in handed[stage]]
+
+    def box(stage, mask, j):
+        return rows(boxes.index((stage, mask)) * count + j, tokens)
+
+    def trade(stage, mask, j):
+        at = (stage * t.members + mask) * count + j
+        if stage == 0:
+            src = part.at[rows(handed[0].index(mask) * count + j, tokens)]
+        else:
+            src = sums.at[rows((stage - 1) * count + j, tokens)]
+        return send_to(src, inbox.at[box(stage, mask, j)], tsend.at[at], trecv.at[at],
+                       t.mate_device(order[stage]))
+
+    def total(ref, base, mask, j, upto):
+        g, h = t.place(j)
+        lows = [(boxes.index((stage, mask ^ order[stage])) * count + j) * per_chunk
+                for stage in range(upto)]
+        first = ((g * t.members + (t.m ^ mask)) * heads + h) * per_chunk
+
+        def strip(b, carry):
+            x = acc[rows(first + b + 1, BLOCK)]
+            for q in range(groups):
+                x = x + extra[table[q, 1, first + b]]
+            for k in range(GLOBALS):
+                x = x + extra[table[0, 2 + k, first + b]]
+            for low in lows:
+                x = x + inbox[rows(low + b, BLOCK)].astype(jnp.float32)
+            ref[rows(base * per_chunk + b, BLOCK)] = x.astype(jnp.bfloat16)
+            return carry
+
+        lax.fori_loop(0, per_chunk, strip, 0)
+
+    js = list(range(1, count)) + [0]
+    for j in js:
+        for mask in reversed(handed[0]):
+            total(part, handed[0].index(mask) * count + j, mask, j, 0)
+            trade(0, mask, j).start()
+    for stage in range(1, len(order)):
+        for j in js:
+            for mask in handed[stage]:
+                for before in range(stage):
+                    trade(before, mask ^ order[before], j).wait_recv()
+                total(sums, (stage - 1) * count + j, mask, j, stage)
+                trade(stage, mask, j).start()
+    for j in js:
+        for stage in range(len(order)):
+            trade(stage, order[stage], j).wait_recv()
+        total(final, j, 0, j, len(order))
+        for a in (2, 3):
+            (back(a, j) if j else back_keep(a)).start()
+    for stage in stages:
+        for mask in masks(stage):
+            for j in range(count):
+                forward(stage, mask, j, True).wait_send()
+        for mask in handed[stage]:
+            for j in js:
+                trade(stage, mask, j).wait_send()
+    for c in idm:
+        c.wait_send()
+    for a in range(4):
+        back_keep(a).wait()
+        for j in range(1, count):
+            move(a, j).wait_send()
+            back(a, j).wait_send()
+            returned(a, j).wait_recv()
+
+
+def grouped(n, heads, groups, query_rows, key_rows, value_rows, out_grad, random_blocks,
+            global_blocks):
+    bf = jnp.bfloat16
+    tokens, full = query_rows.shape
+    members = n // groups
+    count = groups * heads
+    everything = n * heads * tokens
+    held = count * tokens
+    bits = members.bit_length() - 1
+    run = heads * tokens // BLOCK
+    requests = RANDOM * run
+    dma = pltpu.SemaphoreType.DMA
+    sds = jax.ShapeDtypeStruct
+    total = n * run
+    blank = groups * requests + GLOBALS
+    span = -(-max(total, requests) // 128) * 128
+    flat = random_blocks.reshape(requests)
+    names = jnp.arange(total, dtype=jnp.int32)
+    base = (lax.axis_index("seq") // members) * requests - blank
+    slots = base + jnp.arange(requests, dtype=jnp.int32)
+    found = jnp.sum(jnp.where(flat[None, :] == names[:, None], slots[None, :], 0), axis=1) + blank
+    shared = [jnp.where(global_blocks[k] == names, groups * requests + k, blank)
+              for k in range(GLOBALS)]
+    lines = [jnp.pad(x.astype(jnp.int32), (0, span - x.shape[0])) for x in [flat, found] + shared]
+    ids = jnp.pad(jnp.stack(lines), ((0, 8 - len(lines)), (0, 0)))
+    blocked = (tokens // BLOCK, BLOCK, full)
+    key_rows, value_rows = key_rows.reshape(blocked), value_rows.reshape(blocked)
+    query_rows, key_rows, value_rows, out_grad = (
+        pltpu.with_memory_space_constraint(x, pltpu.HBM)
+        for x in (query_rows, key_rows, value_rows, out_grad)
+    )
+    f32 = jnp.float32
+    results = pl.pallas_call(
+        partial(kernel_all, n, heads, groups),
+        out_shape=(sds((tokens, full), bf),) * 4,
+        in_specs=[SMEM] + [HBM] * 4 + [VMEM],
+        out_specs=(VMEM,) * 4,
+        scratch_shapes=[
+            pltpu.VMEM((total + 2, BLOCK, WIDE), bf), pltpu.VMEM((held, WIDE), bf),
+            pltpu.VMEM((held, WIDE), bf), pltpu.VMEM((everything + 2 * BLOCK, WIDE), f32),
+            pltpu.VMEM((groups * requests + GLOBALS + 1, BLOCK, WIDE), f32),
+            pltpu.VMEM((PARTS, BLOCK, WIDE), bf), pltpu.VMEM((groups, 8, span), jnp.int32),
+            pltpu.SMEM((groups, 8, span), jnp.int32),
+            pltpu.VMEM((members // 2 * held, WIDE), bf),
+            pltpu.VMEM(((members - 1) * held, WIDE), bf),
+            pltpu.VMEM((max(bits - 1, 1) * held, WIDE), bf), pltpu.VMEM((held, WIDE), bf),
+            dma((4 * count,)), dma((4 * count,)), dma((6,)),
+            dma((bits * members * count,)), dma((bits * members * count,)),
+            dma((groups,)), dma((groups,)),
+            dma((4 * count,)), dma((4 * count,)), dma((4,)),
+            dma((bits * members * count,)), dma((bits * members * count,)),
+        ],
+        compiler_params=pltpu.CompilerParams(
+            collective_id=0, has_side_effects=True, vmem_limit_bytes=44 * 1024 * 1024
+        ),
+        name="everything",
+    )(global_blocks, key_rows, value_rows, query_rows, out_grad, ids)
+    return pl.pallas_call(
+        kernel_store,
+        out_shape=(sds((tokens, full), bf),) * 4,
+        in_specs=[VMEM] * 4,
+        out_specs=(HBM,) * 4,
+        scratch_shapes=[dma((4,))],
+        compiler_params=pltpu.CompilerParams(vmem_limit_bytes=16 * 1024 * 1024),
+        name="store",
+    )(*results)
+
+
+def chosen(n, heads, query_rows, *others):
+    tokens, full = query_rows.shape
+    groups = full // LANES // heads
+    fits = n * heads * tokens * WIDE * 6 <= 24 * 1024 * 1024
+    if full % (LANES * heads) == 0 and n % groups == 0 and fits and n // groups in (2, 4):
+        return grouped(n, heads, groups, query_rows, *others)
+    return body(n, heads, query_rows, *others)
+
+
 def solution(mesh):
     rows_spec = P(("seq", "head"), None)
     return jax.shard_map(
-        partial(body, mesh.shape["seq"], mesh.shape["head"]),
+        partial(chosen, mesh.shape["seq"], mesh.shape["head"]),
         mesh=mesh,
         in_specs=(rows_spec,) * 4 + (P("seq", None), P()),
         out_specs=(rows_spec,) * 4,

time: 151 us -> 121 us (0.80)
  Pallas kernels: 148 us -> 117 us
    pallas_call x5 -> x2, Pallas kernels: 148 us -> 117 us  [the longest x1 115 us: grouped(): pl.pallas_call(partial(kernel_all, n, heads, groups), out_shape=(sds((tok...]
where the time goes in v2:
time: 121 us
  Pallas kernels  117 us (97%)
  local copies, waits for them, and re-layouts  2.08 us (2%)
  other arithmetic  1.41 us (1%)
    pallas_call x1, Pallas kernels, grouped(): pl.pallas_call(partial(kernel_all, n, heads, groups), out_shape=(sds((tok...  115 us

profile of v2, /device:TPU:0, one launch (start us, length us, event | category | flops | bytes accessed | tf_op | source)
XLA Modules:
  0.0 120.7 jit_solution(7940972296920823252)
XLA Ops:
  0.7 0.0 copy-start
  0.7 0.6 copy-done
  1.3 0.6 fusion
  1.9 1.3 %compare_select_fusion = (s32[1,128]{1,0:T(1,128)S(1)}, s32[1,128]{1,0:T(1,128)S(1)}) fusion(s32[]{:T(128)} %bitcast.5, s32[]{:T(128)} %bitcast.4), kind=kLoop, calls=%fused_computation.3 | loop fusion | flops 512 | bytes 1032 | tf_op jit(solution)/shard_map/jit(_where)/select_n | solution.py:908
  3.2 0.0 copy-start.1
  3.2 0.7 copy-done.1
  3.9 0.1 copy.12
  4.0 0.1 reshape.53
  4.0 0.1 select_reduce_fusion
  4.2 115.2 %everything.1 = (bf16[256,1024]{1,0:T(8,128)(2,1)S(1)}, bf16[256,1024]{1,0:T(8,128)(2,1)S(1)}, bf16[256,1024]{1,0:T(8,128)(2,1)S(1)}, bf16[256,1024]{1,0:T(8,128)(2,1)S(1)}) custom-call(s32[2]{0:T(128)S(1)} %copy-done, bf16[4,64,1024]{2,1,0:T(8,128)(2,1)} %bitcast.8, bf16[4,64,1024]{2,1,0:T(8,128)(2,1)} %bitcast.9, bf16[256,1024]{1,0:T(8,128)(2,1)} %query.1, ...), custom_call_target="tpu_custom_call" | custom-call | tf_op jit(solution)/shard_map/everything/pallas_call | solution.py:919
  119.4 1.3 %store.1 = (bf16[256,1024]{1,0:T(8,128)(2,1)}, bf16[256,1024]{1,0:T(8,128)(2,1)}, bf16[256,1024]{1,0:T(8,128)(2,1)}, bf16[256,1024]{1,0:T(8,128)(2,1)}) custom-call(bf16[256,1024]{1,0:T(8,128)(2,1)S(1)} %get-tuple-element.8.a, bf16[256,1024]{1,0:T(8,128)(2,1)S(1)} %get-tuple-element.9.b, bf16[256,1024]{1,0:T(8,128)(2,1)S(1)} %get-tuple-element.10.c, ...), custom_call_target="tpu_custom_call" | custom-call | tf_op jit(solution)/shard_map/store/pallas_call | solution.py:944
  (4 shorter events, 0.0 us)
Async XLA Ops:
  0.7 0.7 copy-start
  3.2 0.7 copy-start.1

commit v3 on v2

--- a/solution.py
+++ b/solution.py
@@ -560,7 +560,7 @@
     def near(self, i):
         total = self.g * 0
         for g in range(self.groups):
-            order = sorted(range(self.groups), key=lambda k: (abs(k - g), k))
+            order = sorted(range(self.groups), key=lambda k: (k != g, -abs(k - g), k))
             total = total + jnp.where(self.g == g, order[i], 0)
         return total
 
@@ -608,8 +608,8 @@
     )
 
 
-def kernel_all(n, heads, groups, owners, key, value, query, grad, ids, out, qout, kout, vout,
-               kv, qd, od, acc, extra, keys, ids_all, table, part, inbox, sums, final, send, recv,
+def kernel_all(n, heads, groups, named, owners, key, value, query, grad, out, qout, kout, vout,
+               kv, qd, od, acc, extra, keys, ids, ids_all, table, part, inbox, sums, final, send, recv,
                local, fsend, frecv, isend, irecv, bsend, brecv, blocal, tsend, trecv):
     tokens = query.shape[0]
     t = Team(n, heads, groups, tokens)
@@ -617,6 +617,17 @@
     per_chunk = tokens // BLOCK
     run = heads * per_chunk
     requests = RANDOM * run
+    blank = groups * requests + GLOBALS
+    lane = lax.broadcasted_iota(jnp.int32, ids.shape, 1)
+    row = lax.broadcasted_iota(jnp.int32, ids.shape, 0)
+    entry = jnp.where(row == 0, 0, blank)
+    for r in range(requests):
+        name = named[r // RANDOM, r % RANDOM]
+        entry = jnp.where((row == 0) & (lane == r), name, entry)
+        entry = jnp.where((row == 1) & (lane == name), t.g * requests + r, entry)
+    for k in range(GLOBALS):
+        entry = jnp.where((row == 2 + k) & (lane == owners[k]), groups * requests + k, entry)
+    ids[...] = entry
     t.greet()
     arrays = (key, value, query, grad)
     dests = (out, qout, kout, vout)
@@ -656,12 +667,14 @@
                    t.device(t.near(i), t.h)) for i in range(1, groups)]
     for a in (0, 1):
         keep(a).start()
-        for j in range(1, count):
+    for j in range(1, count):
+        for a in (0, 1):
             move(a, j).start()
     start(idm)
     for a in (2, 3):
         keep(a).start()
-        for j in range(1, count):
+    for j in range(1, count):
+        for a in (2, 3):
             move(a, j).start()
     own = pltpu.make_async_copy(ids, ids_all.at[t.g], local.at[4])
     own.start()
@@ -678,12 +691,12 @@
 
     lax.fori_loop(0, acc.shape[0] // BLOCK, clear, 0)
 
-    def forward(stage, mask, j, mine):
+    def forward(stage, mask, p, mine):
         bit = t.bits[stage]
-        g, h = t.place(j)
+        g, h = t.place(p // 2)
         owner = t.m ^ mask if mine else t.m ^ bit ^ mask
-        ref = kv.at[blocks_of(g, h, owner)]
-        at = (stage * t.members + mask) * count + j
+        ref = kv.at[blocks_of(g, h, owner), :, lanes(p)]
+        at = (stage * t.members + mask) * 2 * count + p
         return send_to(ref, ref, fsend.at[at], frecv.at[at], t.mate_device(bit))
 
     def masks(stage):
@@ -693,20 +706,20 @@
         return got
 
     stages = range(len(t.bits))
-    for step in range(count + len(t.bits)):
+    pieces = 2 * count
+    for step in range(pieces + 4 * len(t.bits)):
         for stage in reversed(stages):
-            j = step - stage - 1
-            if 0 <= j < count:
+            p = step - 4 * (stage + 1)
+            if 0 <= p < pieces:
                 for mask in masks(stage):
-                    forward(stage, mask, j, False).wait_recv()
+                    forward(stage, mask, p, False).wait_recv()
                     for later in range(stage + 1, len(t.bits)):
-                        forward(later, mask ^ t.bits[stage], j, True).start()
-        if step < count:
-            for a in (0, 1):
-                if step == 0:
-                    keep(a).wait()
-                else:
-                    arrived(a, step).wait_recv()
+                        forward(later, mask ^ t.bits[stage], p, True).start()
+        if step < pieces:
+            if step < 2:
+                keep(step).wait()
+            else:
+                arrived(step % 2, step // 2).wait_recv()
             for stage in stages:
                 forward(stage, 0, step, True).start()
     own.wait()
@@ -869,8 +882,8 @@
             (back(a, j) if j else back_keep(a)).start()
     for stage in stages:
         for mask in masks(stage):
-            for j in range(count):
-                forward(stage, mask, j, True).wait_send()
+            for p in range(2 * count):
+                forward(stage, mask, p, True).wait_send()
         for mask in handed[stage]:
             for j in js:
                 trade(stage, mask, j).wait_send()
@@ -898,17 +911,7 @@
     dma = pltpu.SemaphoreType.DMA
     sds = jax.ShapeDtypeStruct
     total = n * run
-    blank = groups * requests + GLOBALS
     span = -(-max(total, requests) // 128) * 128
-    flat = random_blocks.reshape(requests)
-    names = jnp.arange(total, dtype=jnp.int32)
-    base = (lax.axis_index("seq") // members) * requests - blank
-    slots = base + jnp.arange(requests, dtype=jnp.int32)
-    found = jnp.sum(jnp.where(flat[None, :] == names[:, None], slots[None, :], 0), axis=1) + blank
-    shared = [jnp.where(global_blocks[k] == names, groups * requests + k, blank)
-              for k in range(GLOBALS)]
-    lines = [jnp.pad(x.astype(jnp.int32), (0, span - x.shape[0])) for x in [flat, found] + shared]
-    ids = jnp.pad(jnp.stack(lines), ((0, 8 - len(lines)), (0, 0)))
     blocked = (tokens // BLOCK, BLOCK, full)
     key_rows, value_rows = key_rows.reshape(blocked), value_rows.reshape(blocked)
     query_rows, key_rows, value_rows, out_grad = (
@@ -919,19 +922,20 @@
     results = pl.pallas_call(
         partial(kernel_all, n, heads, groups),
         out_shape=(sds((tokens, full), bf),) * 4,
-        in_specs=[SMEM] + [HBM] * 4 + [VMEM],
+        in_specs=[SMEM] * 2 + [HBM] * 4,
         out_specs=(VMEM,) * 4,
         scratch_shapes=[
             pltpu.VMEM((total + 2, BLOCK, WIDE), bf), pltpu.VMEM((held, WIDE), bf),
             pltpu.VMEM((held, WIDE), bf), pltpu.VMEM((everything + 2 * BLOCK, WIDE), f32),
             pltpu.VMEM((groups * requests + GLOBALS + 1, BLOCK, WIDE), f32),
-            pltpu.VMEM((PARTS, BLOCK, WIDE), bf), pltpu.VMEM((groups, 8, span), jnp.int32),
+            pltpu.VMEM((PARTS, BLOCK, WIDE), bf), pltpu.VMEM((8, span), jnp.int32),
+            pltpu.VMEM((groups, 8, span), jnp.int32),
             pltpu.SMEM((groups, 8, span), jnp.int32),
             pltpu.VMEM((members // 2 * held, WIDE), bf),
             pltpu.VMEM(((members - 1) * held, WIDE), bf),
             pltpu.VMEM((max(bits - 1, 1) * held, WIDE), bf), pltpu.VMEM((held, WIDE), bf),
             dma((4 * count,)), dma((4 * count,)), dma((6,)),
-            dma((bits * members * count,)), dma((bits * members * count,)),
+            dma((2 * bits * members * count,)), dma((2 * bits * members * count,)),
             dma((groups,)), dma((groups,)),
             dma((4 * count,)), dma((4 * count,)), dma((4,)),
             dma((bits * members * count,)), dma((bits * members * count,)),
@@ -940,7 +944,7 @@
             collective_id=0, has_side_effects=True, vmem_limit_bytes=44 * 1024 * 1024
         ),
         name="everything",
-    )(global_blocks, key_rows, value_rows, query_rows, out_grad, ids)
+    )(random_blocks, global_blocks, key_rows, value_rows, query_rows, out_grad)
     return pl.pallas_call(
         kernel_store,
         out_shape=(sds((tokens, full), bf),) * 4,

time: 121 us -> 108 us (0.89)
  the two profiles are of different devices: /device:TPU:0 before, /device:TPU:24 now
where the time goes in v3:
time: 108 us
  Pallas kernels  106 us (98%)
  local copies, waits for them, and re-layouts  1.33 us (1%)
    pallas_call x1, Pallas kernels, grouped(): pl.pallas_call(partial(kernel_all, n, heads, groups), out_shape=(sds((tok...  104 us

profile of v3, /device:TPU:24, one launch (start us, length us, event | category | flops | bytes accessed | tf_op | source)
XLA Modules:
  0.0 107.6 jit_solution(3933981932914190148)
XLA Ops:
  0.6 0.0 copy-start.1
  0.6 0.7 copy-done.1
  1.3 0.0 copy-start
  1.3 0.1 copy.10.named
  1.4 0.6 copy-done
  2.0 104.3 %everything.1 = (bf16[256,1024]{1,0:T(8,128)(2,1)S(1)}, bf16[256,1024]{1,0:T(8,128)(2,1)S(1)}, bf16[256,1024]{1,0:T(8,128)(2,1)S(1)}, bf16[256,1024]{1,0:T(8,128)(2,1)S(1)}) custom-call(s32[8,2]{1,0:T(8,128)S(1)} %copy.10.named, s32[2]{0:T(128)S(1)} %copy-done, bf16[4,64,1024]{2,1,0:T(8,128)(2,1)} %bitcast.2, bf16[4,64,1024]{2,1,0:T(8,128)(2,1)} %bitcast.3, ...), custom_call_target="tpu_custom_call" | custom-call | tf_op jit(solution)/shard_map/everything/pallas_call | solution.py:922
  106.3 1.3 %store.1 = (bf16[256,1024]{1,0:T(8,128)(2,1)}, bf16[256,1024]{1,0:T(8,128)(2,1)}, bf16[256,1024]{1,0:T(8,128)(2,1)}, bf16[256,1024]{1,0:T(8,128)(2,1)}) custom-call(bf16[256,1024]{1,0:T(8,128)(2,1)S(1)} %get-tuple-element.8.a, bf16[256,1024]{1,0:T(8,128)(2,1)S(1)} %get-tuple-element.9.b, bf16[256,1024]{1,0:T(8,128)(2,1)S(1)} %get-tuple-element.10.c, ...), custom_call_target="tpu_custom_call" | custom-call | tf_op jit(solution)/shard_map/store/pallas_call | solution.py:948
Async XLA Ops:
  0.6 0.7 copy-start.1
  1.3 0.7 copy-start

commit v4 on v3

--- a/solution.py
+++ b/solution.py
@@ -608,8 +608,8 @@
     )
 
 
-def kernel_all(n, heads, groups, named, owners, key, value, query, grad, out, qout, kout, vout,
-               kv, qd, od, acc, extra, keys, ids, ids_all, table, part, inbox, sums, final, send, recv,
+def kernel_all(n, heads, groups, named_in, owners_in, key, value, query, grad, out, qout, kout, vout,
+               kv, qd, od, acc, extra, keys, ids, ids_all, table, named, owners, part, inbox, sums, final, send, recv,
                local, fsend, frecv, isend, irecv, bsend, brecv, blocal, tsend, trecv):
     tokens = query.shape[0]
     t = Team(n, heads, groups, tokens)
@@ -618,16 +618,9 @@
     run = heads * per_chunk
     requests = RANDOM * run
     blank = groups * requests + GLOBALS
-    lane = lax.broadcasted_iota(jnp.int32, ids.shape, 1)
-    row = lax.broadcasted_iota(jnp.int32, ids.shape, 0)
-    entry = jnp.where(row == 0, 0, blank)
-    for r in range(requests):
-        name = named[r // RANDOM, r % RANDOM]
-        entry = jnp.where((row == 0) & (lane == r), name, entry)
-        entry = jnp.where((row == 1) & (lane == name), t.g * requests + r, entry)
-    for k in range(GLOBALS):
-        entry = jnp.where((row == 2 + k) & (lane == owners[k]), groups * requests + k, entry)
-    ids[...] = entry
+    asks = [pltpu.make_async_copy(named_in, named, local.at[6]),
+            pltpu.make_async_copy(owners_in, owners, local.at[7])]
+    start(asks)
     t.greet()
     arrays = (key, value, query, grad)
     dests = (out, qout, kout, vout)
@@ -670,6 +663,29 @@
     for j in range(1, count):
         for a in (0, 1):
             move(a, j).start()
+    wait(asks)
+    lane = lax.broadcasted_iota(jnp.int32, ids.shape, 1)
+    row = lax.broadcasted_iota(jnp.int32, ids.shape, 0)
+    entry = jnp.where(row == 0, 0, blank)
+    for r in range(requests):
+        name = named[r % RANDOM, r // RANDOM]
+        entry = jnp.where((row == 0) & (lane == r), name, entry)
+        entry = jnp.where((row == 1) & (lane == name), t.g * requests + r, entry)
+    for k in range(GLOBALS):
+        entry = jnp.where((row == 2 + k) & (lane == owners[k]), groups * requests + k, entry)
+    ids[...] = entry
+    edge = jnp.zeros(kv.shape[1:], kv.dtype)
+    kv[0] = edge
+    kv[kv.shape[0] - 1] = edge
+    empty = jnp.zeros((BLOCK, WIDE), jnp.float32)
+    for k in range(GLOBALS + 1):
+        extra[groups * requests + k] = empty
+
+    def clear(i, carry):
+        acc[rows(i, BLOCK)] = empty
+        return carry
+
+    lax.fori_loop(0, acc.shape[0] // BLOCK, clear, 0)
     start(idm)
     for a in (2, 3):
         keep(a).start()
@@ -678,18 +694,6 @@
             move(a, j).start()
     own = pltpu.make_async_copy(ids, ids_all.at[t.g], local.at[4])
     own.start()
-    edge = jnp.zeros(kv.shape[1:], kv.dtype)
-    kv[0] = edge
-    kv[kv.shape[0] - 1] = edge
-    empty = jnp.zeros((BLOCK, WIDE), jnp.float32)
-    for k in range(GLOBALS + 1):
-        extra[groups * requests + k] = empty
-
-    def clear(i, carry):
-        acc[rows(i, BLOCK)] = empty
-        return carry
-
-    lax.fori_loop(0, acc.shape[0] // BLOCK, clear, 0)
 
     def forward(stage, mask, p, mine):
         bit = t.bits[stage]
@@ -912,6 +916,8 @@
     sds = jax.ShapeDtypeStruct
     total = n * run
     span = -(-max(total, requests) // 128) * 128
+    picked = pltpu.with_memory_space_constraint(random_blocks.T, pltpu.HBM)
+    shared = pltpu.with_memory_space_constraint(global_blocks, pltpu.HBM)
     blocked = (tokens // BLOCK, BLOCK, full)
     key_rows, value_rows = key_rows.reshape(blocked), value_rows.reshape(blocked)
     query_rows, key_rows, value_rows, out_grad = (
@@ -922,7 +928,7 @@
     results = pl.pallas_call(
         partial(kernel_all, n, heads, groups),
         out_shape=(sds((tokens, full), bf),) * 4,
-        in_specs=[SMEM] * 2 + [HBM] * 4,
+        in_specs=[HBM] * 6,
         out_specs=(VMEM,) * 4,
         scratch_shapes=[
             pltpu.VMEM((total + 2, BLOCK, WIDE), bf), pltpu.VMEM((held, WIDE), bf),
@@ -931,10 +937,11 @@
             pltpu.VMEM((PARTS, BLOCK, WIDE), bf), pltpu.VMEM((8, span), jnp.int32),
             pltpu.VMEM((groups, 8, span), jnp.int32),
             pltpu.SMEM((groups, 8, span), jnp.int32),
+            pltpu.SMEM((RANDOM, run), jnp.int32), pltpu.SMEM((GLOBALS,), jnp.int32),
             pltpu.VMEM((members // 2 * held, WIDE), bf),
             pltpu.VMEM(((members - 1) * held, WIDE), bf),
             pltpu.VMEM((max(bits - 1, 1) * held, WIDE), bf), pltpu.VMEM((held, WIDE), bf),
-            dma((4 * count,)), dma((4 * count,)), dma((6,)),
+            dma((4 * count,)), dma((4 * count,)), dma((8,)),
             dma((2 * bits * members * count,)), dma((2 * bits * members * count,)),
             dma((groups,)), dma((groups,)),
             dma((4 * count,)), dma((4 * count,)), dma((4,)),
@@ -944,7 +951,7 @@
             collective_id=0, has_side_effects=True, vmem_limit_bytes=44 * 1024 * 1024
         ),
         name="everything",
-    )(random_blocks, global_blocks, key_rows, value_rows, query_rows, out_grad)
+    )(picked, shared, key_rows, value_rows, query_rows, out_grad)
     return pl.pallas_call(
         kernel_store,
         out_shape=(sds((tokens, full), bf),) * 4,

time: 108 us -> 106 us (0.981)
  local copies, waits for them, and re-layouts: 1.33 us -> 0 us
    unnamed x5 -> x0, local copies, waits for them, and re-layouts: 1.33 us -> none
where the time goes in v4:
time: 106 us
  Pallas kernels  105 us (99%)
    pallas_call x1, Pallas kernels, grouped(): pl.pallas_call(partial(kernel_all, n, heads, groups), out_shape=(sds((tok...  104 us

profile of v4, /device:TPU:24, one launch (start us, length us, event | category | flops | bytes accessed | tf_op | source)
XLA Modules:
  0.0 105.7 jit_solution(17622171756679493429)
XLA Ops:
  0.6 103.7 %everything.1 = (bf16[256,1024]{1,0:T(8,128)(2,1)S(1)}, bf16[256,1024]{1,0:T(8,128)(2,1)S(1)}, bf16[256,1024]{1,0:T(8,128)(2,1)S(1)}, bf16[256,1024]{1,0:T(8,128)(2,1)S(1)}) custom-call(s32[2,8]{1,0:T(2,128)} %bitcast.5, s32[2]{0:T(128)} %owners_in.1, bf16[4,64,1024]{2,1,0:T(8,128)(2,1)} %bitcast.3, bf16[4,64,1024]{2,1,0:T(8,128)(2,1)} %bitcast.4, ...), custom_call_target="tpu_custom_call" | custom-call | tf_op jit(solution)/shard_map/everything/pallas_call | solution.py:928
  104.3 1.3 %store.1 = (bf16[256,1024]{1,0:T(8,128)(2,1)}, bf16[256,1024]{1,0:T(8,128)(2,1)}, bf16[256,1024]{1,0:T(8,128)(2,1)}, bf16[256,1024]{1,0:T(8,128)(2,1)}) custom-call(bf16[256,1024]{1,0:T(8,128)(2,1)S(1)} %get-tuple-element.8.a, bf16[256,1024]{1,0:T(8,128)(2,1)S(1)} %get-tuple-element.9.b, bf16[256,1024]{1,0:T(8,128)(2,1)S(1)} %get-tuple-element.10.c, ...), custom_call_target="tpu_custom_call" | custom-call | tf_op jit(solution)/shard_map/store/pallas_call | solution.py:955

commit v5 on v4

--- a/solution.py
+++ b/solution.py
@@ -560,7 +560,7 @@
     def near(self, i):
         total = self.g * 0
         for g in range(self.groups):
-            order = sorted(range(self.groups), key=lambda k: (k != g, -abs(k - g), k))
+            order = sorted(range(self.groups), key=lambda k: (k != g, -abs(k - g), -abs(2 * k + 1 - self.groups)))
             total = total + jnp.where(self.g == g, order[i], 0)
         return total
 
@@ -867,17 +867,28 @@
         lax.fori_loop(0, per_chunk, strip, 0)
 
     js = list(range(1, count)) + [0]
-    for j in js:
-        for mask in reversed(handed[0]):
-            total(part, handed[0].index(mask) * count + j, mask, j, 0)
-            trade(0, mask, j).start()
-    for stage in range(1, len(order)):
-        for j in js:
-            for mask in handed[stage]:
-                for before in range(stage):
-                    trade(before, mask ^ order[before], j).wait_recv()
-                total(sums, (stage - 1) * count + j, mask, j, stage)
-                trade(stage, mask, j).start()
+    def hand(mask, j):
+        total(part, handed[0].index(mask) * count + j, mask, j, 0)
+        trade(0, mask, j).start()
+
+    def relay(stage, j):
+        for mask in handed[stage]:
+            for before in range(stage):
+                trade(before, mask ^ order[before], j).wait_recv()
+            total(sums, (stage - 1) * count + j, mask, j, stage)
+            trade(stage, mask, j).start()
+
+    early = [x for x in handed[0] if x & ~order[0]]
+    late = [x for x in handed[0] if not x & ~order[0]]
+    for i in range(count + 2):
+        if i < count:
+            for mask in early:
+                hand(mask, js[i])
+        if i >= 2:
+            for stage in range(1, len(order)):
+                relay(stage, js[i - 2])
+            for mask in late:
+                hand(mask, js[i - 2])
     for j in js:
         for stage in range(len(order)):
             trade(stage, order[stage], j).wait_recv()

time: 106 us -> 103 us (0.972)
  the two profiles are of different devices: /device:TPU:24 before, /device:TPU:0 now
where the time goes in v5:
time: 103 us; the launch traced here: 102 us
  Pallas kernels  102 us (99%)
    pallas_call x1, Pallas kernels, grouped(): pl.pallas_call(partial(kernel_all, n, heads, groups), out_shape=(sds((tok...  100 us

profile of v5, /device:TPU:0, one launch (start us, length us, event | category | flops | bytes accessed | tf_op | source)
XLA Modules:
  0.0 102.4 jit_solution(5107764138104782904)
XLA Ops:
  0.6 100.4 %everything.1 = (bf16[256,1024]{1,0:T(8,128)(2,1)S(1)}, bf16[256,1024]{1,0:T(8,128)(2,1)S(1)}, bf16[256,1024]{1,0:T(8,128)(2,1)S(1)}, bf16[256,1024]{1,0:T(8,128)(2,1)S(1)}) custom-call(s32[2,8]{1,0:T(2,128)} %bitcast.5, s32[2]{0:T(128)} %owners_in.1, bf16[4,64,1024]{2,1,0:T(8,128)(2,1)} %bitcast.3, bf16[4,64,1024]{2,1,0:T(8,128)(2,1)} %bitcast.4, ...), custom_call_target="tpu_custom_call" | custom-call | tf_op jit(solution)/shard_map/everything/pallas_call | solution.py:939
  101.0 1.3 %store.1 = (bf16[256,1024]{1,0:T(8,128)(2,1)}, bf16[256,1024]{1,0:T(8,128)(2,1)}, bf16[256,1024]{1,0:T(8,128)(2,1)}, bf16[256,1024]{1,0:T(8,128)(2,1)}) custom-call(bf16[256,1024]{1,0:T(8,128)(2,1)S(1)} %get-tuple-element.8.a, bf16[256,1024]{1,0:T(8,128)(2,1)S(1)} %get-tuple-element.9.b, bf16[256,1024]{1,0:T(8,128)(2,1)S(1)} %get-tuple-element.10.c, ...), custom_call_target="tpu_custom_call" | custom-call | tf_op jit(solution)/shard_map/store/pallas_call | solution.py:966
